TPU v7x, 256 devices: a whole 4x4x8 slice. The times are simulated.
256 devices in a mesh: dp: 64 (over x, z, core), rep: 4 (over y).
Axes of the slice: x: 4, y: 4, z: 8, core: 2. Of those that a mesh axis runs over, the one named last changes fastest.
Arguments:
- frames_in: bfloat16 [4, 57344, 1536], P('rep', 'dp')
- lengths: int32 [4, 64, 4], P('rep', 'dp'), may hold values from 1 to 893, as said below
- norm_gain: float32 [1536], replicated, may hold values from 0.5 to 1.5
- norm_bias: float32 [1536], replicated, may hold values from -2 to 2
- w_in: bfloat16 [1536, 3072], P(('dp', 'rep')), may hold values from -0.15625 to 0.15625
- kernel: float32 [31, 1536], replicated, may hold values from -1 to 1
- batch_gain: float32 [1536], replicated, may hold values from 0.5 to 1.5
- batch_bias: float32 [1536], replicated, may hold values from -3 to 3
- w_out: bfloat16 [1536, 1536], P(('dp', 'rep')), may hold values from -0.15625 to 0.15625
Outputs:
- frames_out: bfloat16 [4, 57344, 1536], P('rep', 'dp')
Inputs may be any that keep to these rules, and one draw needn't show every extreme that they name: `lengths`: for each rep index, the devices 2k and 2k + 1 of dp hold 1024 frames together, so each rep index holds 512 frames for each of its dp devices; a device holds at most 896 frames, and some device of every rep index holds exactly 896.
All inputs are finite; a program needn't handle non-finite values.
Results may differ from a plain program's by a relative error of at most 0.0038.
Values may be sent and summed in bfloat16 or wider, within the bound.
A program may use at most 128 MiB of HBM per device.

v0:
```python
import jax
import jax.numpy as jnp
from jax import lax
from jax.sharding import PartitionSpec as P

FR_DEV = 512
EPSILON = 1e-05


def layer_norm(frames, norm_gain, norm_bias):
    values = frames.astype(jnp.float32)
    average = jnp.mean(values, axis=-1, keepdims=True)
    centred = values - average
    spread = jnp.mean(centred * centred, axis=-1, keepdims=True)
    return centred * lax.rsqrt(spread + EPSILON) * norm_gain + norm_bias


def depthwise(gated, labels, kernel):
    half_kernel = kernel.shape[0] // 2
    length_rows = gated.shape[0]
    padded = jnp.pad(gated, ((half_kernel, half_kernel), (0, 0)))
    padded_labels = jnp.pad(labels, (half_kernel, half_kernel), constant_values=-1)
    summed = jnp.zeros(gated.shape, jnp.float32)
    for offset in range(kernel.shape[0]):
        shared = padded_labels[offset : offset + length_rows] == labels
        contribution = jnp.where(
            shared[:, None], padded[offset : offset + length_rows].astype(jnp.float32), 0.0
        )
        summed = summed + contribution * kernel[offset]
    return summed


def project_in(normed, weight_rows):
    return jnp.dot(normed, weight_rows, preferred_element_type=jnp.float32)


def project_out(active, weight_rows):
    return jnp.dot(active, weight_rows, preferred_element_type=jnp.float32)


def on_device(
    frames_in, lengths, norm_gain, norm_bias, w_in, kernel, batch_gain, batch_bias, w_out
):
    local_frames = frames_in[0]
    local_lengths = lengths[0, 0]
    capacity = local_frames.shape[0]
    features = local_frames.shape[1]
    total_count = lax.axis_size("dp") * lax.axis_size("rep") * FR_DEV
    grouped = (w_in, w_out)
    grouped = (
        lax.all_gather(w_in, ("dp", "rep"), axis=0, tiled=True),
        lax.all_gather(w_out, ("dp", "rep"), axis=0, tiled=True),
    )
    rows_here = jnp.arange(capacity, dtype=jnp.int32)
    local_load = jnp.sum(local_lengths)
    bounds = jnp.cumsum(local_lengths)
    labels = jnp.sum((rows_here[:, None] >= bounds[None, :]).astype(jnp.int32), axis=1)
    row_weight = (rows_here < local_load).astype(jnp.float32)[:, None]
    normed = layer_norm(local_frames, norm_gain, norm_bias).astype(jnp.bfloat16)
    projected = project_in(normed, grouped[0])
    gated = (projected[:, :features] * jax.nn.sigmoid(projected[:, features:])).astype(jnp.bfloat16)
    convolved = depthwise(gated, labels, kernel)
    average = lax.psum(jnp.sum(convolved * row_weight, axis=0), ("dp", "rep")) / total_count
    centred = convolved - average
    spread = lax.psum(jnp.sum(centred * centred * row_weight, axis=0), ("dp", "rep")) / total_count
    scaled = centred * lax.rsqrt(spread + EPSILON) * batch_gain + batch_bias
    active = jax.nn.silu(scaled).astype(jnp.bfloat16)
    branch = project_out(active, grouped[1])
    mixed = (local_frames.astype(jnp.float32) + branch).astype(jnp.bfloat16)
    result = jnp.where(rows_here[:, None] < local_load, mixed, jnp.zeros_like(mixed))
    return result[None]


def solution(mesh):
    placed = (
        P("rep", "dp", None),
        P("rep", "dp", None),
        P(),
        P(),
        P(("dp", "rep"), None),
        P(),
        P(),
        P(),
        P(("dp", "rep"), None),
    )
    return jax.shard_map(
        on_device, mesh=mesh, in_specs=placed, out_specs=P("rep", "dp", None), check_vma=False
    )
```

profile of v0, /device:TPU:1, one launch (start us, length us, event | category | flops | bytes accessed | tf_op | source)
XLA Modules:
  0.0 487.7 jit_solution(4124133330554323458)
XLA Ops:
  6.5 0.0 all-gather.7.cloned.1.call-start
  6.5 0.7 all-gather.7.cloned.1.call-update
  7.3 0.0 all-gather.5.cloned.1.call-start
  7.3 0.7 all-gather.5.cloned.1.call-update
  8.0 1.3 reduce_sum.54
  9.3 0.8 reduce-window.8
  10.1 0.6 iota_compare_fusion.1
  10.8 0.7 fusion.26
  11.4 0.1 convert_reduce_fusion.1
  11.5 1.5 slice_reduce_fusion.29
  13.0 1.8 slice_reduce_fusion.30
  14.9 0.1 slice_compare_fusion.26
  14.9 2.2 convert_reduce_fusion
  17.2 2.6 fusion.4
  19.8 0.1 slice_compare_fusion.29
  19.9 0.1 slice_compare_fusion.28
  20.0 0.1 slice_compare_fusion.27
  20.1 111.2 %all-gather.7.cloned.1.call-done = bf16[256,6,1536]{2,1,0:T(8,128)(2,1)} async-done(((bf16[1,6,1536]{2,1,0:T(8,128)(2,1)}), bf16[256,6,1536]{2,1,0:T(8,128)(2,1)}) %all-gather.7.cloned.1.call-update) | async-done | bytes 4718608 | tf_op jit(solution)/shard_map/all_gather | solution.py:52
  131.3 8.5 %reshape.87 = bf16[1536,1536]{1,0:T(8,128)(2,1)} reshape(bf16[256,6,1536]{2,1,0:T(8,128)(2,1)} %all-gather.7.cloned.1.call-done) | data formatting | bytes 9437184
  139.8 0.0 copy-start
  139.8 0.0 copy-start.2
  139.8 0.0 copy-start.3
  139.8 113.5 %all-gather.5.cloned.1.call-done = bf16[256,6,3072]{2,1,0:T(8,128)(2,1)} async-done(((bf16[1,6,3072]{2,1,0:T(8,128)(2,1)}), bf16[256,6,3072]{2,1,0:T(8,128)(2,1)}) %all-gather.5.cloned.1.call-update) | async-done | bytes 9437200 | tf_op jit(solution)/shard_map/all_gather | solution.py:51
  253.3 14.2 %reshape.85 = bf16[1536,3072]{1,0:T(8,128)(2,1)} reshape(bf16[256,6,3072]{2,1,0:T(8,128)(2,1)} %all-gather.5.cloned.1.call-done) | data formatting | bytes 18874368
  267.5 0.0 copy-done
  267.5 0.0 copy-done.2
  267.5 0.0 copy-done.3
  267.5 11.3 %fusion.16 = f32[896,3072]{1,0:T(8,128)S(1)} fusion(bf16[1536,3072]{1,0:T(8,128)(2,1)} %reshape.85, bf16[1,896,1536]{2,1,0:T(8,128)(2,1)S(1)} %copy-done, f32[1536]{0:T(1024)S(1)} %copy-done.2, f32[1536]{0:T(1024)S(1)} %copy-done.3, f32[896]{0:T(1024)S(1)} %add_rsqrt_fusion.1, f32[896]{0:T(1024)S(1)} %broadcast_multiply_fusion.1), kind=kOutput, calls=%fused_computation.23 | convolution fusion | flops 8463974400 | bytes 23219200 | tf_op jit(solution)/shard_map/dot_general | solution.py:34
  278.8 1.5 fusion.13
  280.4 0.0 copy-start.4
  280.4 0.0 copy-start.5
  280.4 38.3 %multiply_reduce_fusion.1 = (f32[1536]{0:T(1024)S(1)}, f32[896,1536]{1,0:T(8,128)}) fusion(f32[896]{0:T(1024)S(1)} %fusion.26, f32[1536]{0:T(1024)S(1)} %get-tuple-element.34, pred[896]{0:T(1024)(128)(4,1)S(1)} %get-tuple-element.67, f32[1536]{0:T(1024)S(1)} %get-tuple-element.35, pred[896]{0:T(1024)(128)(4,1)S(1)} %get-tuple-element.39, ...), kind=kLoop, calls=%fused_computation.18 | loop fusion | flops 170654208 | bytes 8484608 | tf_op jit(solution)/shard_map/reduce_sum | solution.py:63
  318.7 0.0 copy-start.1
  318.7 74.8 %psum.14 = f32[1536]{0:T(1024)S(1)} all-reduce(f32[1536]{0:T(1024)S(1)} %get-tuple-element.36), channel_id=1, replica_groups=mesh['dp'=64,'rep'=4] {'dp','rep'}, use_global_device_ids=true, to_apply=%region_6.7 | all-reduce | flops 1536 | bytes 12288 | tf_op jit(solution)/shard_map/psum | solution.py:63
  393.5 3.3 multiply_reduce_fusion
  396.8 73.6 %psum.15 = f32[1536]{0:T(1024)S(1)} all-reduce(f32[1536]{0:T(1024)S(1)} %multiply_reduce_fusion), channel_id=1, replica_groups=mesh['dp'=64,'rep'=4] {'dp','rep'}, use_global_device_ids=true, to_apply=%region_8.9 | all-reduce | flops 1536 | bytes 12288 | tf_op jit(solution)/shard_map/psum | solution.py:65
  470.4 0.0 copy-done.4
  470.4 0.0 copy-done.5
  470.4 0.0 copy-done.1
  470.4 10.4 %fusion.15 = bf16[1,896,1536]{2,1,0:T(8,128)(2,1)} fusion(bf16[1536,1536]{1,0:T(8,128)(2,1)} %reshape.87, bf16[1,896,1536]{2,1,0:T(8,128)(2,1)S(1)} %copy-done.1, f32[896,1536]{1,0:T(8,128)} %get-tuple-element.37, f32[1536]{0:T(1024)S(1)} %copy-done.4, f32[1536]{0:T(1024)S(1)} %copy-done.5, f32[1536]{0:T(1024)S(1)} %add_rsqrt_fusion, ...), kind=kOutput, calls=%fused_computation.22 | convolution fusion | flops 4245749760 | bytes 15754112 | tf_op jit(solution)/shard_map/dot_general | solution.py:38
  (4 shorter events, 0.0 us)
Async XLA Ops:
  6.5 124.8 %all-gather.7.cloned.1.call-start = ((), (), s32[]{:S(2)}) async-start(), calls=%async_computation.1 | async-start | bytes 6316032 | tf_op jit(solution)/shard_map/all_gather | solution.py:52
  7.3 246.1 %all-gather.5.cloned.1.call-start = ((), (), s32[]{:S(2)}) async-start(), calls=%async_computation | async-start | bytes 12632064 | tf_op jit(solution)/shard_map/all_gather | solution.py:51
  139.8 127.7 %copy-start = (bf16[1,896,1536]{2,1,0:T(8,128)(2,1)S(1)}, bf16[1,896,1536]{2,1,0:T(8,128)(2,1)}, u32[]{:S(2)}) copy-start(bf16[1,896,1536]{2,1,0:T(8,128)(2,1)} %param.9) | copy-start | bytes 8257540
  139.8 127.7 %copy-start.2 = (f32[1536]{0:T(1024)S(1)}, f32[1536]{0:T(1024)}, u32[]{:S(2)}) copy-start(f32[1536]{0:T(1024)} %param.12) | copy-start | bytes 18436
  139.8 127.7 %copy-start.3 = (f32[1536]{0:T(1024)S(1)}, f32[1536]{0:T(1024)}, u32[]{:S(2)}) copy-start(f32[1536]{0:T(1024)} %param.11) | copy-start | bytes 18436
  280.4 190.1 %copy-start.4 = (f32[1536]{0:T(1024)S(1)}, f32[1536]{0:T(1024)}, u32[]{:S(2)}) copy-start(f32[1536]{0:T(1024)} %param.16) | copy-start | bytes 18436
  280.4 190.1 %copy-start.5 = (f32[1536]{0:T(1024)S(1)}, f32[1536]{0:T(1024)}, u32[]{:S(2)}) copy-start(f32[1536]{0:T(1024)} %param.15) | copy-start | bytes 18436
  318.7 151.7 %copy-start.1 = (bf16[1,896,1536]{2,1,0:T(8,128)(2,1)S(1)}, bf16[1,896,1536]{2,1,0:T(8,128)(2,1)}, u32[]{:S(2)}) copy-start(bf16[1,896,1536]{2,1,0:T(8,128)(2,1)} %param.9) | copy-start | bytes 8257540
Sparse Core Ops, SparseCore 0:
  11.2 120.0 all-gather.6
  135.1 118.1 all-gather.4
where the time goes:
time: 489 us; the launch traced here: 488 us
  waiting for transfers between devices  226 us (46%)
  blocking collectives  148 us (30%)
  other arithmetic  51.8 us (11%)
  local copies, waits for them, and re-layouts  26 us (5%)
  matrix products  21.8 us (4%)
  between operations  13.5 us (3%)
    all_gather x1, waiting for transfers between devices, on_device(): lax.all_gather(w_in, ('dp', 'rep'), axis=0, tiled=True)  114 us
    all_gather x1, waiting for transfers between devices, on_device(): lax.all_gather(w_out, ('dp', 'rep'), axis=0, tiled=True)  111 us
    psum x1, blocking collectives, on_device(): lax.psum(jnp.sum(convolved * row_weight, axis=0), ('dp', 'rep'))  74.8 us
    psum x1, blocking collectives, on_device(): lax.psum(jnp.sum(centred * centred * row_weight, axis=0), ('dp', 'rep'))  73.6 us
    reduce_sum x1, other arithmetic, on_device(): jnp.sum(convolved * row_weight, axis=0)  38.3 us
    unnamed x14, local copies, waits for them, and re-layouts  22.6 us
    dot_general x1, matrix products, project_in(): return jnp.dot(normed, weight_rows, preferred_element_type=jnp.float32)  11.3 us
    dot_general x1, matrix products, project_out(): return jnp.dot(active, weight_rows, preferred_element_type=jnp.float32)  10.4 us
  transfers between devices with their start and end apart: 2, of which 2 were waited for; matrix products, arithmetic and copies ran while one was open for 4% of the time, Pallas kernels for 0%

commit v1 on v0

--- a/solution.py
+++ b/solution.py
@@ -48,7 +48,10 @@
     total_count = lax.axis_size("dp") * lax.axis_size("rep") * FR_DEV
     grouped = (w_in, w_out)
     grouped = (
-        lax.all_gather(w_in, ("dp", "rep"), axis=0, tiled=True),
+        jnp.concatenate(
+            lax.all_to_all(jnp.stack([w_in] * lax.axis_size(("dp", "rep"))), ("dp", "rep"), 0, 0),
+            axis=0,
+        ),
         lax.all_gather(w_out, ("dp", "rep"), axis=0, tiled=True),
     )
     rows_here = jnp.arange(capacity, dtype=jnp.int32)

time: 489 us -> 555 us (1.13)
  waiting for transfers between devices: 226 us -> 278 us
  starting transfers between devices: 0.04 us -> 16.6 us
    all_to_all x0 -> x1, waiting for transfers between devices: none -> 130 us  [on_device(): lax.all_to_all(jnp.stack([w_in] * lax.axis_size(('dp', 'rep'))), ('dp', '...]
    all_gather x1 -> x0, waiting for transfers between devices: 114 us -> none  [on_device(): lax.all_gather(w_in, ('dp', 'rep'), axis=0, tiled=True)]
    all_gather x1, waiting for transfers between devices: 111 us -> 147 us  [on_device(): lax.all_gather(w_out, ('dp', 'rep'), axis=0, tiled=True)]
    all_to_all x0 -> x1, starting transfers between devices: none -> 16.5 us  [on_device(): lax.all_to_all(jnp.stack([w_in] * lax.axis_size(('dp', 'rep'))), ('dp', '...]
    unnamed x14 -> x17, local copies, waits for them, and re-layouts: 22.6 us -> 8.43 us
    reshape x0 -> x1, local copies, waits for them, and re-layouts: none -> 14.2 us  [on_device(): jnp.concatenate(lax.all_to_all(jnp.stack([w_in] * lax.axis_size(('dp', 'r...]
    another operation x0 -> x1, local copies, waits for them, and re-layouts: none -> 6.86 us  [on_device(): jnp.stack([w_in] * lax.axis_size(('dp', 'rep')))]
  transfers between devices with their start and end apart: 2 -> 2, of which waited for: 2 -> 2; matrix products, arithmetic and copies ran while one was open for 4% -> 2% of each run, Pallas kernels for 0% -> 0%
where the time goes in v1:
time: 555 us; the launch traced here: 554 us
  waiting for transfers between devices  278 us (50%)
  blocking collectives  147 us (26%)
  other arithmetic  46.9 us (8%)
  local copies, waits for them, and re-layouts  30 us (5%)
  matrix products  21.8 us (4%)
  starting transfers between devices  16.6 us (3%)
  between operations  13.5 us (2%)
    all_gather x1, waiting for transfers between devices, on_device(): lax.all_gather(w_out, ('dp', 'rep'), axis=0, tiled=True)  147 us
    all_to_all x1, waiting for transfers between devices, on_device(): lax.all_to_all(jnp.stack([w_in] * lax.axis_size(('dp', 'rep'))), ('dp', '...  130 us
    psum x1, blocking collectives, on_device(): lax.psum(jnp.sum(centred * centred * row_weight, axis=0), ('dp', 'rep'))  74.3 us
    psum x1, blocking collectives, on_device(): lax.psum(jnp.sum(convolved * row_weight, axis=0), ('dp', 'rep'))  72.6 us
    reduce_sum x1, other arithmetic, on_device(): jnp.sum(convolved * row_weight, axis=0)  38.2 us
    all_to_all x1, starting transfers between devices, on_device(): lax.all_to_all(jnp.stack([w_in] * lax.axis_size(('dp', 'rep'))), ('dp', '...  16.5 us
    reshape x1, local copies, waits for them, and re-layouts, on_device(): jnp.concatenate(lax.all_to_all(jnp.stack([w_in] * lax.axis_size(('dp', 'r...  14.2 us
    dot_general x1, matrix products, project_in(): return jnp.dot(normed, weight_rows, preferred_element_type=jnp.float32)  11.3 us
  transfers between devices with their start and end apart: 2, of which 2 were waited for; matrix products, arithmetic and copies ran while one was open for 2% of the time, Pallas kernels for 0%

profile of v1, /device:TPU:1, one launch (start us, length us, event | category | flops | bytes accessed | tf_op | source)
XLA Modules:
  0.0 553.9 jit_solution(557869866906929020)
XLA Ops:
  6.5 6.9 %stack.2 = bf16[256,6,3072]{2,1,0:T(8,128)(2,1)} broadcast(bf16[6,3072]{1,0:T(8,128)(2,1)} %param.13), dimensions={1,2} | broadcast | bytes 9474048 | tf_op jit(solution)/shard_map/stack | solution.py:52
  13.4 0.0 copy-start.7
  13.4 0.0 copy-start.2
  13.4 0.0 copy-start
  13.4 16.5 %all-to-all-start = ((bf16[256,6,3072]{2,1,0:T(8,128)(2,1)}), bf16[256,6,3072]{2,1,0:T(8,128)(2,1)}, u32[]{:S(2)}, u32[]{:S(2)}) async-start(bf16[256,6,3072]{2,1,0:T(8,128)(2,1)} %stack.2), calls=%async_computation | async-start | bytes 25165824 | tf_op jit(solution)/shard_map/all_to_all | solution.py:52
  29.9 0.0 all-gather.3.cloned.1.call-start
  30.0 0.7 all-gather.3.cloned.1.call-update
  30.7 0.0 copy-done.7
  30.7 0.6 reduce_sum.54
  31.3 0.2 reduce-window.8
  31.5 0.6 iota_compare_fusion.1
  32.2 0.7 fusion.27
  32.8 0.1 convert_reduce_fusion.1
  32.9 0.0 copy-done.2
  32.9 0.2 slice_reduce_fusion.29
  33.1 0.3 slice_reduce_fusion.30
  33.4 0.1 slice_compare_fusion.26
  33.5 0.0 copy-done
  33.5 0.4 convert_reduce_fusion
  34.0 0.9 fusion.3
  34.8 0.1 slice_compare_fusion.29
  34.9 0.1 slice_compare_fusion.28
  35.0 0.1 slice_compare_fusion.27
  35.1 147.1 %all-gather.3.cloned.1.call-done = bf16[256,6,1536]{2,1,0:T(8,128)(2,1)} async-done(((bf16[1,6,1536]{2,1,0:T(8,128)(2,1)}), bf16[256,6,1536]{2,1,0:T(8,128)(2,1)}) %all-gather.3.cloned.1.call-update) | async-done | bytes 4718608 | tf_op jit(solution)/shard_map/all_gather | solution.py:55
  182.2 8.4 %reshape.118 = bf16[1536,1536]{1,0:T(8,128)(2,1)} reshape(bf16[256,6,1536]{2,1,0:T(8,128)(2,1)} %all-gather.3.cloned.1.call-done) | data formatting | bytes 9437184
  190.6 0.0 copy-start.3
  190.6 0.0 copy-start.4
  190.6 130.3 %all-to-all-done = bf16[256,6,3072]{2,1,0:T(8,128)(2,1)} async-done(((bf16[256,6,3072]{2,1,0:T(8,128)(2,1)}), bf16[256,6,3072]{2,1,0:T(8,128)(2,1)}, u32[]{:S(2)}, u32[]{:S(2)}) %all-to-all-start) | async-done | bytes 9437216 | tf_op jit(solution)/shard_map/all_to_all | solution.py:52
  321.0 14.2 %reshape.116 = bf16[1536,3072]{1,0:T(8,128)(2,1)} reshape(bf16[256,6,3072]{2,1,0:T(8,128)(2,1)} %all-to-all-done) | data formatting | bytes 18874368 | tf_op jit(solution)/shard_map/reshape | solution.py:51
  335.2 0.0 copy-done.3
  335.2 0.0 copy-done.4
  335.2 11.3 %fusion.17 = f32[896,3072]{1,0:T(8,128)S(1)} fusion(bf16[1536,3072]{1,0:T(8,128)(2,1)} %reshape.116, bf16[1,896,1536]{2,1,0:T(8,128)(2,1)S(1)} %copy-done, f32[1536]{0:T(1024)S(1)} %copy-done.3, f32[1536]{0:T(1024)S(1)} %copy-done.4, f32[896]{0:T(1024)S(1)} %add_rsqrt_fusion.1, f32[896]{0:T(1024)S(1)} %broadcast_multiply_fusion.1), kind=kOutput, calls=%fused_computation.25 | convolution fusion | flops 8463974400 | bytes 23219200 | tf_op jit(solution)/shard_map/dot_general | solution.py:34
  346.5 1.5 fusion.13
  348.0 0.0 copy-start.5
  348.0 0.0 copy-start.6
  348.1 38.2 %multiply_reduce_fusion.1 = (f32[1536]{0:T(1024)S(1)}, f32[896,1536]{1,0:T(8,128)}) fusion(f32[896]{0:T(1024)S(1)} %fusion.27, f32[1536]{0:T(1024)S(1)} %get-tuple-element.34, pred[896]{0:T(1024)(128)(4,1)S(1)} %get-tuple-element.67, f32[1536]{0:T(1024)S(1)} %get-tuple-element.35, pred[896]{0:T(1024)(128)(4,1)S(1)} %get-tuple-element.39, ...), kind=kLoop, calls=%fused_computation.19 | loop fusion | flops 170654208 | bytes 8484608 | tf_op jit(solution)/shard_map/reduce_sum | solution.py:66
  386.3 0.0 copy-start.1
  386.3 72.6 %psum.14 = f32[1536]{0:T(1024)S(1)} all-reduce(f32[1536]{0:T(1024)S(1)} %get-tuple-element.36), channel_id=1, replica_groups=mesh['dp'=64,'rep'=4] {'dp','rep'}, use_global_device_ids=true, to_apply=%region_6.7 | all-reduce | flops 1536 | bytes 12288 | tf_op jit(solution)/shard_map/psum | solution.py:66
  458.9 3.3 multiply_reduce_fusion
  462.2 74.3 %psum.15 = f32[1536]{0:T(1024)S(1)} all-reduce(f32[1536]{0:T(1024)S(1)} %multiply_reduce_fusion), channel_id=1, replica_groups=mesh['dp'=64,'rep'=4] {'dp','rep'}, use_global_device_ids=true, to_apply=%region_8.9 | all-reduce | flops 1536 | bytes 12288 | tf_op jit(solution)/shard_map/psum | solution.py:68
  536.5 0.0 copy-done.5
  536.5 0.0 copy-done.6
  536.5 0.0 copy-done.1
  536.6 10.5 %fusion.15 = bf16[1,896,1536]{2,1,0:T(8,128)(2,1)} fusion(bf16[1536,1536]{1,0:T(8,128)(2,1)} %reshape.118, bf16[1,896,1536]{2,1,0:T(8,128)(2,1)S(1)} %copy-done.1, f32[896,1536]{1,0:T(8,128)} %get-tuple-element.37, f32[1536]{0:T(1024)S(1)} %copy-done.5, f32[1536]{0:T(1024)S(1)} %copy-done.6, f32[1536]{0:T(1024)S(1)} %add_rsqrt_fusion, ...), kind=kOutput, calls=%fused_computation.23 | convolution fusion | flops 4245749760 | bytes 15754112 | tf_op jit(solution)/shard_map/dot_general | solution.py:38
  (4 shorter events, 0.0 us)
Async XLA Ops:
  13.4 17.3 %copy-start.7 = (s32[1,1,4]{2,1,0:T(1,128)S(1)}, s32[1,1,4]{2,1,0:T(1,128)}, u32[]{:S(2)}) copy-start(s32[1,1,4]{2,1,0:T(1,128)} %param.10) | copy-start | bytes 52
  13.4 19.5 %copy-start.2 = (f32[31,1536]{1,0:T(8,128)S(1)}, f32[31,1536]{1,0:T(8,128)}, u32[]{:S(2)}) copy-start(f32[31,1536]{1,0:T(8,128)} %param.14) | copy-start | bytes 571396
  13.4 20.1 %copy-start = (bf16[1,896,1536]{2,1,0:T(8,128)(2,1)S(1)}, bf16[1,896,1536]{2,1,0:T(8,128)(2,1)}, u32[]{:S(2)}) copy-start(bf16[1,896,1536]{2,1,0:T(8,128)(2,1)} %param.9) | copy-start | bytes 8257540
  13.4 307.6 %all-to-all-start = ((bf16[256,6,3072]{2,1,0:T(8,128)(2,1)}), bf16[256,6,3072]{2,1,0:T(8,128)(2,1)}, u32[]{:S(2)}, u32[]{:S(2)}) async-start(bf16[256,6,3072]{2,1,0:T(8,128)(2,1)} %stack.2), calls=%async_computation | async-start | bytes 25165824 | tf_op jit(solution)/shard_map/all_to_all | solution.py:52
  29.9 152.3 %all-gather.3.cloned.1.call-start = ((), (), s32[]{:S(2)}) async-start(), calls=%async_computation.1 | async-start | bytes 6316032 | tf_op jit(solution)/shard_map/all_gather | solution.py:55
  190.6 144.5 %copy-start.3 = (f32[1536]{0:T(1024)S(1)}, f32[1536]{0:T(1024)}, u32[]{:S(2)}) copy-start(f32[1536]{0:T(1024)} %param.12) | copy-start | bytes 18436
  190.6 144.5 %copy-start.4 = (f32[1536]{0:T(1024)S(1)}, f32[1536]{0:T(1024)}, u32[]{:S(2)}) copy-start(f32[1536]{0:T(1024)} %param.11) | copy-start | bytes 18436
  348.0 188.5 %copy-start.5 = (f32[1536]{0:T(1024)S(1)}, f32[1536]{0:T(1024)}, u32[]{:S(2)}) copy-start(f32[1536]{0:T(1024)} %param.16) | copy-start | bytes 18436
  348.0 188.5 %copy-start.6 = (f32[1536]{0:T(1024)S(1)}, f32[1536]{0:T(1024)}, u32[]{:S(2)}) copy-start(f32[1536]{0:T(1024)} %param.15) | copy-start | bytes 18436
  386.3 150.3 %copy-start.1 = (bf16[1,896,1536]{2,1,0:T(8,128)(2,1)S(1)}, bf16[1,896,1536]{2,1,0:T(8,128)(2,1)}, u32[]{:S(2)}) copy-start(bf16[1,896,1536]{2,1,0:T(8,128)(2,1)} %param.9) | copy-start | bytes 8257540
Sparse Core Ops, SparseCore 0:
  34.6 147.5 all-gather.2
